TPU v7x, 512 devices: a whole 4x8x8 slice. The times are simulated.
512 devices in a mesh: fsdp: 32 (over z, y_hi), tensor: 16 (over x, y_lo, core).
Axes of the slice: x: 4, y: 8 (y_hi: 4, y_lo: 2; y = y_hi * 2 + y_lo), z: 8, core: 2. Of those that a mesh axis runs over, the one named last changes fastest.
Arguments:
- old_codes: bfloat16 [26624, 16384], P(('fsdp', 'tensor')), may hold values from -1 to 1
- old_scales: float32 [208, 128], replicated, may hold values from 0.003 to 0.03
- gate_pre: bfloat16 [2048, 26624], P('fsdp', 'tensor'), may hold values from -6 to 6
- up_pre: bfloat16 [2048, 26624], P('fsdp', 'tensor'), may hold values from -6 to 6
Outputs:
- mixed: bfloat16 [2048, 16384], P('tensor', 'fsdp')
- codes_t: bfloat16 [16384, 26624], P('fsdp', 'tensor')
- scales_t: float32 [128, 208], P('fsdp', 'tensor')
All inputs are finite; a program needn't handle non-finite values. Where the computation divides by a largest or mean magnitude, that divisor is 1e-20 or more.
Results may differ from a plain program's by a relative error of at most 0.024.
Values may be sent and summed in bfloat16 or wider, within the bound.
No kernel may reach another device: no remote copies, remote signals or barrier semaphores. Data moves between devices by JAX's collectives and lax.ppermute only.
A program may use at most 64 MiB of HBM per device.

v0:
```python
import jax
import jax.numpy as jnp
from jax import lax
from jax.sharding import PartitionSpec as P

TILE = 128
epsilon = 1e-06


def regroup(moved, senders, per_owner, block_rows, col_width):
    stacked = moved.reshape(senders, per_owner, block_rows, col_width)
    return jnp.swapaxes(stacked, 0, 1).reshape(senders * per_owner * block_rows, col_width)


def body(old_codes, old_scales, gate_pre, up_pre):
    n_fsdp = lax.axis_size("fsdp")
    n_tensor = lax.axis_size("tensor")
    f_index = lax.axis_index("fsdp")
    t_index = lax.axis_index("tensor")
    block_rows, full_width = old_codes.shape
    col_width = full_width // n_fsdp
    col_tiles = col_width // TILE
    per_owner = n_fsdp // n_tensor
    own_rows = block_rows * n_fsdp
    row_tiles = own_rows // TILE
    hidden = (jax.nn.silu(gate_pre.astype(jnp.float32)) * up_pre.astype(jnp.float32)).astype(
        jnp.bfloat16
    )
    sectioned = lax.all_to_all(old_codes, "fsdp", split_axis=1, concat_axis=0, tiled=True)
    scale_cols = lax.dynamic_slice_in_dim(old_scales, f_index * col_tiles, col_tiles, 1)
    moved = lax.all_to_all(
        sectioned.reshape(n_tensor, per_owner * block_rows, col_width),
        "tensor",
        split_axis=0,
        concat_axis=0,
        tiled=True,
    )
    final_rows = regroup(moved, n_tensor, per_owner, block_rows, col_width)
    scale_block = lax.dynamic_slice_in_dim(scale_cols, t_index * row_tiles, row_tiles, 0)
    tile_values = (
        final_rows.astype(jnp.float32).reshape(row_tiles, TILE, col_tiles, TILE)
        * scale_block[:, None, :, None]
    )
    new_scale = jnp.max(jnp.abs(tile_values), axis=(1, 3)) + epsilon
    new_codes = (tile_values / new_scale[:, None, :, None]).astype(jnp.bfloat16)
    weight = (
        (new_codes.astype(jnp.float32) * new_scale[:, None, :, None])
        .astype(jnp.bfloat16)
        .reshape(own_rows, col_width)
    )
    partial_value = jnp.dot(
        lax.all_gather(hidden, "fsdp", axis=0, tiled=True),
        weight,
        preferred_element_type=jnp.float32,
    )
    codes_t = new_codes.reshape(own_rows, col_width).T
    scales_t = new_scale.T
    mixed = lax.psum_scatter(
        partial_value.astype(jnp.bfloat16), "tensor", scatter_dimension=0, tiled=True
    )
    return (mixed, codes_t, scales_t)


def solution(mesh):
    return jax.shard_map(
        body,
        mesh=mesh,
        in_specs=(P(("fsdp", "tensor"), None), P(), P("fsdp", "tensor"), P("fsdp", "tensor")),
        out_specs=(P("tensor", "fsdp"), P("fsdp", "tensor"), P("fsdp", "tensor")),
        check_vma=False,
    )
```

profile of v0, /device:TPU:16, one launch (start us, length us, event | category | flops | bytes accessed | tf_op | source)
XLA Modules:
  0.0 263.3 jit_solution(17682116257781332109)
XLA Ops:
  7.2 0.0 all-gather.2.cloned.1.call-start
  7.2 1.8 fusion.7
  9.1 0.0 all-gather.2.cloned.1.call-update
  9.1 2.2 copy.20
  11.2 0.2 slice
  11.4 0.9 copy.14
  12.4 74.0 %all_to_all.21 = bf16[52,32,512]{2,0,1:T(8,128)(2,1)S(1)} all-to-all(bf16[52,32,512]{2,0,1:T(8,128)(2,1)S(1)} %copy.14), channel_id=1, replica_groups=mesh['fsdp'=32,'tensor'=16] {'fsdp'}, dimensions={1} | all-to-all | bytes 3407872 | tf_op jit(solution)/shard_map/all_to_all | solution.py:29
  86.4 1.3 reshape.38
  87.7 4.3 %all-to-all-start.1 = ((bf16[16,104,512]{2,1,0:T(8,128)(2,1)}), bf16[16,104,512]{2,1,0:T(8,128)(2,1)S(1)}, u32[]{:S(2)}, u32[]{:S(2)}) async-start(bf16[16,104,512]{2,1,0:T(8,128)(2,1)} %reshape.38), calls=%async_computation.1 | async-start | bytes 3407872 | tf_op jit(solution)/shard_map/all_to_all | solution.py:31
  92.0 0.2 reduce-scatter.2.cloned.1.call-start
  92.3 0.8 dynamic_slice.4
  93.1 33.8 %all-to-all-done.1 = bf16[16,104,512]{2,1,0:T(8,128)(2,1)S(1)} async-done(((bf16[16,104,512]{2,1,0:T(8,128)(2,1)}), bf16[16,104,512]{2,1,0:T(8,128)(2,1)S(1)}, u32[]{:S(2)}, u32[]{:S(2)}) %all-to-all-start.1) | async-done | bytes 1703968 | tf_op jit(solution)/shard_map/all_to_all | solution.py:31
  126.9 0.6 copy.15
  127.4 3.8 %copy.16 = f32[2,16,52,512]{3,2,1,0:T(8,128)} copy(f32[2,16,52,512]{3,1,2,0:T(8,128)S(1)} %bitcast.27) | data formatting | bytes 6815744 | tf_op jit(solution)/shard_map/convert_element_type | solution.py:41
  131.3 5.1 %reshape.40 = f32[13,128,4,128]{3,2,1,0:T(4,128)} reshape(f32[2,16,52,512]{3,2,1,0:T(8,128)} %copy.16) | data formatting | bytes 6815744 | tf_op jit(solution)/shard_map/convert_element_type | solution.py:41
  136.4 2.9 %reshape.39 = f32[1664,512]{1,0:T(8,128)S(1)} reshape(f32[2,16,52,512]{3,2,1,0:T(8,128)} %copy.16) | data formatting | bytes 6815744 | tf_op jit(solution)/shard_map/convert_element_type | solution.py:41
  139.3 3.0 %abs_reduce_fusion = f32[13,4]{1,0:T(8,128)S(1)} fusion(f32[13,128,4,128]{3,2,1,0:T(4,128)} %reshape.40, f32[13,4]{1,0:T(8,128)S(1)} %dynamic_slice.4), kind=kLoop, calls=%fused_computation.5 | loop fusion | flops 2555852 | bytes 3408288 | tf_op jit(solution)/shard_map/reduce_max | solution.py:44
  142.3 0.5 div.17
  142.8 0.0 copy-start
  142.8 0.5 mul.38
  143.4 1.3 copy-done
  144.6 2.5 fusion
  147.2 0.0 copy-start.1
  147.2 32.4 %all-gather.2.cloned.1.call-done = bf16[2048,1664]{1,0:T(8,128)(2,1)} async-done(((bf16[64,1664]{1,0:T(8,128)(2,1)}), bf16[2048,1664]{1,0:T(8,128)(2,1)}) %all-gather.2.cloned.1.call-update) | async-done | bytes 6815760 | tf_op jit(solution)/shard_map/all_gather | solution.py:52
  179.5 9.7 %convolution_convert_fusion = bf16[2048,512]{1,0:T(8,128)(2,1)} fusion(bf16[2048,1664]{1,0:T(8,128)(2,1)} %all-gather.2.cloned.1.call-done, bf16[1664,512]{1,0:T(8,128)(2,1)} %fusion, f32[208,8,4,128]{3,2,1,0:T(4,128)} %bitcast.29), kind=kOutput, calls=%fused_computation.6 | convolution fusion | flops 3493265408 | bytes 14024704 | tf_op jit(solution)/shard_map/dot_general | solution.py:51
  189.3 0.0 reduce-scatter.2.cloned.1.call-update
  189.3 0.0 copy-done.1
  189.3 2.3 copy.18
  191.6 0.7 copy.19
  192.3 64.2 %reduce-scatter.2.cloned.1.call-done = bf16[128,512]{1,0:T(8,128)(2,1)} async-done(((bf16[2048,512]{1,0:T(8,128)(2,1)}), bf16[128,512]{1,0:T(8,128)(2,1)}) %reduce-scatter.2.cloned.1.call-update) | async-done | bytes 131088 | tf_op jit(solution)/shard_map/reduce_scatter | solution.py:58
  (1 shorter events, 0.0 us)
Async XLA Ops:
  7.2 172.4 %all-gather.2.cloned.1.call-start = ((), (), s32[]{:S(2)}) async-start(), calls=%async_computation.3 | async-start | bytes 7028736 | tf_op jit(solution)/shard_map/all_gather | solution.py:52
  87.7 39.2 %all-to-all-start.1 = ((bf16[16,104,512]{2,1,0:T(8,128)(2,1)}), bf16[16,104,512]{2,1,0:T(8,128)(2,1)S(1)}, u32[]{:S(2)}, u32[]{:S(2)}) async-start(bf16[16,104,512]{2,1,0:T(8,128)(2,1)} %reshape.38), calls=%async_computation.1 | async-start | bytes 3407872 | tf_op jit(solution)/shard_map/all_to_all | solution.py:31
  92.0 164.5 %reduce-scatter.2.cloned.1.call-start = ((), (), s32[]{:S(2)}) async-start(), calls=%async_computation.4 | async-start | bytes 2228224 | tf_op jit(solution)/shard_map/reduce_scatter | solution.py:58
  142.8 1.8 copy-start
  147.2 42.1 %copy-start.1 = (bf16[1664,512]{1,0:T(8,128)(2,1)S(1)}, bf16[1664,512]{1,0:T(8,128)(2,1)}, u32[]{:S(2)}) copy-start(bf16[1664,512]{1,0:T(8,128)(2,1)} %fusion) | copy-start | bytes 5111812
Sparse Core Ops, SparseCore 0:
  11.2 168.3 all-gather.1
  189.4 67.0 reduce-scatter.1
where the time goes:
time: 264 us; the launch traced here: 263 us
  waiting for transfers between devices  130 us (49%)
  blocking collectives  74 us (28%)
  local copies, waits for them, and re-layouts  23.1 us (9%)
  between operations  14.1 us (5%)
  matrix products  9.71 us (4%)
  other arithmetic  7.42 us (3%)
  starting transfers between devices  4.58 us (2%)
    all_to_all x1, blocking collectives, body(): lax.all_to_all(old_codes, 'fsdp', split_axis=1, concat_axis=0, tiled=True)  74 us
    reduce_scatter x1, waiting for transfers between devices, body(): lax.psum_scatter(partial_value.astype(jnp.bfloat16), 'tensor', scatter_di...  64.2 us
    all_to_all x1, waiting for transfers between devices, body(): lax.all_to_all(sectioned.reshape(n_tensor, per_owner * block_rows, col_wi...  33.8 us
    all_gather x1, waiting for transfers between devices, body(): lax.all_gather(hidden, 'fsdp', axis=0, tiled=True)  32.4 us
    convert_element_type x4, local copies, waits for them, and re-layouts, body(): final_rows.astype(jnp.float32).reshape(row_tiles, TILE, col_tiles, TILE)  12.4 us
    dot_general x1, matrix products, body(): jnp.dot(lax.all_gather(hidden, 'fsdp', axis=0, tiled=True), weight, prefe...  9.71 us
    unnamed x7, local copies, waits for them, and re-layouts  6.44 us
  transfers between devices with their start and end apart: 3, of which 3 were waited for; matrix products, arithmetic and copies ran while one was open for 10% of the time, Pallas kernels for 0%

commit v1 on v0

--- a/solution.py
+++ b/solution.py
@@ -26,7 +26,12 @@
     hidden = (jax.nn.silu(gate_pre.astype(jnp.float32)) * up_pre.astype(jnp.float32)).astype(
         jnp.bfloat16
     )
-    sectioned = lax.all_to_all(old_codes, "fsdp", split_axis=1, concat_axis=0, tiled=True)
+    sectioned = jnp.concatenate(
+        lax.all_to_all(
+            jnp.stack(jnp.split(old_codes, lax.axis_size("fsdp"), axis=1)), "fsdp", 0, 0
+        ),
+        axis=0,
+    )
     scale_cols = lax.dynamic_slice_in_dim(old_scales, f_index * col_tiles, col_tiles, 1)
     moved = lax.all_to_all(
         sectioned.reshape(n_tensor, per_owner * block_rows, col_width),

time: 264 us -> 265 us (level)
  local copies, waits for them, and re-layouts: 23.1 us -> 28.8 us
    unnamed x7 -> x39, local copies, waits for them, and re-layouts: 6.44 us -> 13.2 us
    all_gather x1, waiting for transfers between devices: 32.4 us -> 26.6 us  [body(): lax.all_gather(hidden, 'fsdp', axis=0, tiled=True)]
    all_to_all x1, waiting for transfers between devices: 33.8 us -> 38.5 us  [body(): lax.all_to_all(sectioned.reshape(n_tensor, per_owner * block_rows, col_wi...]
  transfers between devices with their start and end apart: 3 -> 3, of which waited for: 3 -> 3; matrix products, arithmetic and copies ran while one was open for 10% -> 12% of each run, Pallas kernels for 0% -> 0%
where the time goes in v1:
time: 265 us; the launch traced here: 264 us
  waiting for transfers between devices  128 us (48%)
  blocking collectives  71.5 us (27%)
  local copies, waits for them, and re-layouts  28.8 us (11%)
  between operations  14.3 us (5%)
  matrix products  9.71 us (4%)
  other arithmetic  7.54 us (3%)
  starting transfers between devices  4.46 us (2%)
    all_to_all x1, blocking collectives, body(): lax.all_to_all(jnp.stack(jnp.split(old_codes, lax.axis_size('fsdp'), axis...  71.5 us
    reduce_scatter x1, waiting for transfers between devices, body(): lax.psum_scatter(partial_value.astype(jnp.bfloat16), 'tensor', scatter_di...  63 us
    all_to_all x1, waiting for transfers between devices, body(): lax.all_to_all(sectioned.reshape(n_tensor, per_owner * block_rows, col_wi...  38.5 us
    all_gather x1, waiting for transfers between devices, body(): lax.all_gather(hidden, 'fsdp', axis=0, tiled=True)  26.6 us
    unnamed x39, local copies, waits for them, and re-layouts  13.2 us
    convert_element_type x4, local copies, waits for them, and re-layouts, body(): final_rows.astype(jnp.float32).reshape(row_tiles, TILE, col_tiles, TILE)  12.5 us
    dot_general x1, matrix products, body(): jnp.dot(lax.all_gather(hidden, 'fsdp', axis=0, tiled=True), weight, prefe...  9.71 us
  transfers between devices with their start and end apart: 3, of which 3 were waited for; matrix products, arithmetic and copies ran while one was open for 12% of the time, Pallas kernels for 0%

profile of v1, /device:TPU:16, one launch (start us, length us, event | category | flops | bytes accessed | tf_op | source)
XLA Modules:
  0.0 264.5 jit_solution(15389057564141532054)
XLA Ops:
  7.2 0.0 copy-start.2
  7.2 0.0 all-gather.2.cloned.1.call-start
  7.2 2.0 fusion.7
  9.2 0.0 all-gather.2.cloned.1.call-update
  9.2 0.8 constant_dynamic-update-slice_fusion.31
  10.0 0.8 constant_dynamic-update-slice_fusion.30
  10.9 0.8 constant_dynamic-update-slice_fusion.29
  11.7 0.8 constant_dynamic-update-slice_fusion.28
  12.5 0.8 constant_dynamic-update-slice_fusion.27
  13.3 0.8 constant_dynamic-update-slice_fusion.26
  14.2 0.8 constant_dynamic-update-slice_fusion.25
  15.0 0.8 constant_dynamic-update-slice_fusion.24
  15.8 0.8 constant_dynamic-update-slice_fusion.23
  16.6 0.0 copy-done.2
  16.9 71.5 %all_to_all.10 = bf16[32,52,512]{2,1,0:T(8,128)(2,1)S(1)} all-to-all(bf16[32,52,512]{2,1,0:T(8,128)(2,1)S(1)} %constant_dynamic-update-slice_fusion), channel_id=1, replica_groups=mesh['fsdp'=32,'tensor'=16] {'fsdp'}, dimensions={0} | all-to-all | bytes 3407872 | tf_op jit(solution)/shard_map/all_to_all | solution.py:30
  88.5 1.3 reshape_reshape.3
  89.8 4.4 %all-to-all-start.1 = ((bf16[16,104,512]{2,1,0:T(8,128)(2,1)}), bf16[16,104,512]{2,1,0:T(8,128)(2,1)S(1)}, u32[]{:S(2)}, u32[]{:S(2)}) async-start(bf16[16,104,512]{2,1,0:T(8,128)(2,1)} %reshape_reshape.3), calls=%async_computation.1 | async-start | bytes 3407872 | tf_op jit(solution)/shard_map/all_to_all | solution.py:36
  94.2 0.0 reduce-scatter.2.cloned.1.call-start
  94.2 0.8 dynamic_slice.4
  95.0 38.5 %all-to-all-done.1 = bf16[16,104,512]{2,1,0:T(8,128)(2,1)S(1)} async-done(((bf16[16,104,512]{2,1,0:T(8,128)(2,1)}), bf16[16,104,512]{2,1,0:T(8,128)(2,1)S(1)}, u32[]{:S(2)}, u32[]{:S(2)}) %all-to-all-start.1) | async-done | bytes 1703968 | tf_op jit(solution)/shard_map/all_to_all | solution.py:36
  133.6 0.6 copy.13
  134.1 3.8 %copy.14 = f32[2,16,52,512]{3,2,1,0:T(8,128)} copy(f32[2,16,52,512]{3,1,2,0:T(8,128)S(1)} %bitcast.87) | data formatting | bytes 6815744 | tf_op jit(solution)/shard_map/convert_element_type | solution.py:46
  138.0 5.2 %reshape.32 = f32[13,128,4,128]{3,2,1,0:T(4,128)} reshape(f32[2,16,52,512]{3,2,1,0:T(8,128)} %copy.14) | data formatting | bytes 6815744 | tf_op jit(solution)/shard_map/convert_element_type | solution.py:46
  143.1 2.9 %reshape.31 = f32[1664,512]{1,0:T(8,128)S(1)} reshape(f32[2,16,52,512]{3,2,1,0:T(8,128)} %copy.14) | data formatting | bytes 6815744 | tf_op jit(solution)/shard_map/convert_element_type | solution.py:46
  146.0 3.0 %abs_reduce_fusion = f32[13,4]{1,0:T(8,128)S(1)} fusion(f32[13,128,4,128]{3,2,1,0:T(4,128)} %reshape.32, f32[13,4]{1,0:T(8,128)S(1)} %dynamic_slice.4), kind=kLoop, calls=%fused_computation.5 | loop fusion | flops 2555852 | bytes 3408288 | tf_op jit(solution)/shard_map/reduce_max | solution.py:49
  149.1 0.5 div.17
  149.6 0.0 copy-start
  149.6 0.5 mul.38
  150.1 1.3 copy-done
  151.4 2.5 fusion
  153.9 26.6 %all-gather.2.cloned.1.call-done = bf16[2048,1664]{1,0:T(8,128)(2,1)} async-done(((bf16[64,1664]{1,0:T(8,128)(2,1)}), bf16[2048,1664]{1,0:T(8,128)(2,1)}) %all-gather.2.cloned.1.call-update) | async-done | bytes 6815760 | tf_op jit(solution)/shard_map/all_gather | solution.py:57
  180.5 9.7 %convolution_convert_fusion = bf16[2048,512]{1,0:T(8,128)(2,1)} fusion(bf16[2048,1664]{1,0:T(8,128)(2,1)} %all-gather.2.cloned.1.call-done, bf16[1664,512]{1,0:T(8,128)(2,1)} %fusion, f32[208,8,4,128]{3,2,1,0:T(4,128)} %bitcast.89), kind=kOutput, calls=%fused_computation.6 | convolution fusion | flops 3493265408 | bytes 14024704 | tf_op jit(solution)/shard_map/dot_general | solution.py:56
  190.2 0.0 copy-start.1
  190.2 0.0 reduce-scatter.2.cloned.1.call-update
  190.3 1.4 copy-done.1
  191.7 2.3 copy.16
  194.0 0.7 copy.17
  194.7 63.0 %reduce-scatter.2.cloned.1.call-done = bf16[128,512]{1,0:T(8,128)(2,1)} async-done(((bf16[2048,512]{1,0:T(8,128)(2,1)}), bf16[128,512]{1,0:T(8,128)(2,1)}) %reduce-scatter.2.cloned.1.call-update) | async-done | bytes 131088 | tf_op jit(solution)/shard_map/reduce_scatter | solution.py:63
  (24 shorter events, 0.2 us)
Async XLA Ops:
  7.2 9.5 %copy-start.2 = (bf16[52,16384]{1,0:T(8,128)(2,1)S(1)}, bf16[52,16384]{1,0:T(8,128)(2,1)}, u32[]{:S(2)}) copy-start(bf16[52,16384]{1,0:T(8,128)(2,1)} %param.4) | copy-start | bytes 5111812
  7.2 173.3 %all-gather.2.cloned.1.call-start = ((), (), s32[]{:S(2)}) async-start(), calls=%async_computation.3 | async-start | bytes 7028736 | tf_op jit(solution)/shard_map/all_gather | solution.py:57
  89.8 43.8 %all-to-all-start.1 = ((bf16[16,104,512]{2,1,0:T(8,128)(2,1)}), bf16[16,104,512]{2,1,0:T(8,128)(2,1)S(1)}, u32[]{:S(2)}, u32[]{:S(2)}) async-start(bf16[16,104,512]{2,1,0:T(8,128)(2,1)} %reshape_reshape.3), calls=%async_computation.1 | async-start | bytes 3407872 | tf_op jit(solution)/shard_map/all_to_all | solution.py:36
  94.2 163.5 %reduce-scatter.2.cloned.1.call-start = ((), (), s32[]{:S(2)}) async-start(), calls=%async_computation.4 | async-start | bytes 2228224 | tf_op jit(solution)/shard_map/reduce_scatter | solution.py:63
  149.6 1.8 copy-start
  190.2 1.5 copy-start.1
Sparse Core Ops, SparseCore 0:
  11.2 169.3 all-gather.1
  190.4 67.2 reduce-scatter.1
